TPU v7x, 256 devices: a whole 4x4x8 slice. The times are simulated.
256 devices in a mesh: ctx: 32 (over y, z), tp: 8 (over x, core).
Axes of the slice: x: 4, y: 4, z: 8, core: 2. Of those that a mesh axis runs over, the one named last changes fastest.
Arguments:
- q_in: bfloat16 [8192, 8192], P('ctx', 'tp'), may hold values from -10.5 to 10.5
- k_in: bfloat16 [8192, 8192], P('ctx', 'tp'), may hold values from -6 to 6
- v_in: bfloat16 [8192, 8192], P('ctx', 'tp'), may hold values from -6 to 6
- grad_out: bfloat16 [8192, 8192], P('ctx', 'tp'), may hold values from -6 to 6
- doc_ids: int32 [8192], P('ctx'), may hold values from 0 to 3, never falling along the last dimension, each value on 1 to 4096 neighbouring positions
- gain: bfloat16 [8192], P('tp'), may hold values from 0.099609375 to 1.8984375
- filters: bfloat16 [512, 128], P('tp'), may hold values from -0.5 to 0.5
- short_weight: bfloat16 [3, 3, 8192], P(None, None, 'tp'), may hold values from -3.5 to 3.5
Outputs:
- grad_q: bfloat16 [8192, 8192], P('ctx', 'tp')
- grad_k: bfloat16 [8192, 8192], P('ctx', 'tp')
- grad_v: bfloat16 [8192, 8192], P('ctx', 'tp')
- grad_gain: float32 [8192], P('tp')
- grad_filters: float32 [512, 128], P('tp')
- grad_short: float32 [3, 3, 8192], P(None, None, 'tp')
Inputs may be any that keep to these rules, and one draw needn't show every extreme that they name: doc_ids never fall along the window, so every document is one run of consecutive tokens; one document covers exactly 4096 tokens.
All inputs are finite; a program needn't handle non-finite values.
Results may differ from a plain program's by a relative error of at most 0.0049.
Values may be sent and summed in bfloat16 or wider, within the bound.
A program may use at most 128 MiB of HBM per device.

v0:
```python
import math
import jax
import jax.numpy as jnp
from jax import lax
from jax.sharding import PartitionSpec as P

D = 8192
EPS = 1e-06


def shifted(value, axis, by):
    count = lax.axis_size(axis)
    pairs = [(i, i + by) for i in range(count) if 0 <= i + by < count]
    return lax.ppermute(value, axis, pairs)


def featurize(extended, weights, marks_ext, rim_edge):
    length = extended.shape[0] - rim_edge
    own_marks = marks_ext[rim_edge:]
    running = jnp.zeros((length, extended.shape[1]), jnp.float32)
    for offset in range(rim_edge + 1):
        start_row = rim_edge - offset
        agree = (marks_ext[start_row : start_row + length] == own_marks).astype(jnp.float32)[
            :, None
        ]
        running = (
            running
            + weights[offset].astype(jnp.float32)[None, :]
            * extended[start_row : start_row + length].astype(jnp.float32)
            * agree
        )
    return running


def banded(coeffs, block_rows):
    groups, taps = coeffs.shape
    span_cols = block_rows + taps - 1
    padded = jnp.concatenate([coeffs, jnp.zeros((groups, block_rows), coeffs.dtype)], axis=1)
    repeated = jnp.tile(padded, (1, block_rows))[:, : block_rows * span_cols]
    return repeated.reshape(groups, block_rows, span_cols)


def diagonal_sums(pair_grad, taps):
    groups, block_rows, span_cols = pair_grad.shape
    flat_terms = pair_grad.reshape(groups, block_rows * span_cols)
    flat_terms = jnp.concatenate([flat_terms, jnp.zeros((groups, block_rows), jnp.float32)], axis=1)
    return jnp.sum(flat_terms.reshape(groups, block_rows, span_cols + 1)[:, :, :taps], axis=1)


def unfeature(grad_feat, tail, weights, marks_after, own_marks):
    row_count = grad_feat.shape[0]
    extended = jnp.concatenate([grad_feat, tail], axis=0)
    running = jnp.zeros(grad_feat.shape, jnp.float32)
    for offset in range(weights.shape[0]):
        agree = (marks_after[offset : offset + row_count] == own_marks).astype(jnp.float32)[:, None]
        running = (
            running
            + weights[offset].astype(jnp.float32)[None, :]
            * extended[offset : offset + row_count]
            * agree
        )
    return running.astype(jnp.bfloat16)


def short_terms(grad_feat, short_in, short_marks, own_marks, rim_edge):
    row_count = grad_feat.shape[0]
    pieces = []
    for offset in range(rim_edge + 1):
        start_row = rim_edge - offset
        agree = (short_marks[start_row : start_row + row_count] == own_marks).astype(jnp.float32)[
            :, None
        ]
        pieces.append(
            jnp.sum(
                grad_feat * short_in[start_row : start_row + row_count].astype(jnp.float32) * agree,
                axis=0,
            )
        )
    return jnp.stack(pieces)


def on_device(q_in, k_in, v_in, grad_out, doc_ids, gain, filters, short_weight):
    row_count, channels = q_in.shape
    groups, taps = filters.shape
    group_width = channels // groups
    rim_edge = short_weight.shape[1] - 1
    tap_reach = taps - 1
    rim_span = tap_reach + rim_edge
    block_rows = min(row_count, max(128, row_count // 8))
    span_cols = block_rows + tap_reach
    grad_scale = 1.0 / math.sqrt(row_count * lax.axis_size("ctx"))
    doc_marks = doc_ids + 1
    previous = shifted(
        (
            q_in[row_count - rim_edge :],
            k_in[row_count - rim_span :],
            v_in[row_count - rim_span :],
            doc_marks[row_count - rim_span :],
        ),
        "ctx",
        1,
    )
    marks_ext = jnp.concatenate([previous[3], doc_marks], axis=0)
    long_marks = marks_ext[rim_edge:]
    short_marks = marks_ext[tap_reach:]
    q_short = jnp.concatenate([previous[0], q_in], axis=0)
    k_ext = jnp.concatenate([previous[1], k_in], axis=0)
    v_ext = jnp.concatenate([previous[2], v_in], axis=0)
    k_short = k_ext[tap_reach:]
    v_short = v_ext[tap_reach:]
    k_wide = featurize(k_ext, short_weight[1], marks_ext, rim_edge)
    v_wide = featurize(v_ext, short_weight[2], marks_ext, rim_edge)
    product_ext = (k_wide * v_wide).astype(jnp.bfloat16)
    feat_k = k_wide[tap_reach:]
    feat_v = v_wide[tap_reach:]
    feat_q = featurize(q_short, short_weight[0], short_marks, rim_edge)
    forward_band = banded(filters[:, ::-1], block_rows)
    backward_band = banded(filters, block_rows)
    masks = []
    mixed_parts = []
    for start in range(0, row_count, block_rows):
        agree = (
            long_marks[start : start + span_cols][None, :]
            == doc_marks[start : start + block_rows][:, None]
        ).astype(jnp.bfloat16)
        masks.append(agree)
        segment = product_ext[start : start + span_cols].reshape(span_cols, groups, group_width)
        mixed_parts.append(
            jnp.einsum(
                "gij,jgc->igc",
                forward_band * agree[None],
                segment,
                preferred_element_type=jnp.float32,
            ).reshape(block_rows, channels)
        )
    mixed = jnp.concatenate(mixed_parts, axis=0)
    y_out = feat_q * mixed
    weighted = gain.astype(jnp.float32)[None, :] * grad_out.astype(jnp.float32)
    square_sum, inner_sum = lax.psum(
        (jnp.sum(y_out * y_out, axis=1), jnp.sum(weighted * y_out, axis=1)), "tp"
    )
    row_scale = lax.rsqrt(square_sum / D + EPS)
    grad_y = row_scale[:, None] * weighted - y_out * (row_scale**3 * inner_sum / D)[:, None]
    gain_term = (
        jnp.sum(grad_out.astype(jnp.float32) * y_out * row_scale[:, None], axis=0) * grad_scale
    )
    grad_gain = lax.psum(gain_term, "ctx")
    grad_fq = grad_y * mixed
    grad_mixed = (grad_y * feat_q).astype(jnp.bfloat16)
    following = shifted((grad_mixed[:tap_reach], doc_marks[:tap_reach]), "ctx", -1)
    mixed_ext = jnp.concatenate([grad_mixed, following[0]], axis=0)
    marks_after = jnp.concatenate([doc_marks, following[1]], axis=0)
    prod_parts = []
    filter_term = jnp.zeros((groups, taps), jnp.float32)
    for position, start in enumerate(range(0, row_count, block_rows)):
        agree = (
            marks_after[start : start + span_cols][None, :]
            == doc_marks[start : start + block_rows][:, None]
        ).astype(jnp.bfloat16)
        segment = mixed_ext[start : start + span_cols].reshape(span_cols, groups, group_width)
        prod_parts.append(
            jnp.einsum(
                "gij,jgc->igc",
                backward_band * agree[None],
                segment,
                preferred_element_type=jnp.float32,
            ).reshape(block_rows, channels)
        )
        own_block = grad_mixed[start : start + block_rows].reshape(block_rows, groups, group_width)
        behind = product_ext[start : start + span_cols].reshape(span_cols, groups, group_width)
        pair_grad = (
            jnp.einsum("igc,jgc->gij", own_block, behind, preferred_element_type=jnp.float32)
            * masks[position].astype(jnp.float32)[None]
        )
        filter_term = filter_term + diagonal_sums(pair_grad, taps)
    filter_term = filter_term[:, ::-1] * grad_scale
    grad_filters = lax.psum(filter_term, "ctx")
    grad_prod = jnp.concatenate(prod_parts, axis=0)
    grad_fk = grad_prod * feat_v
    grad_fv = grad_prod * feat_k
    tails_after = shifted(
        jnp.stack([grad_fq[:rim_edge], grad_fk[:rim_edge], grad_fv[:rim_edge]]), "ctx", -1
    )
    grad_q = unfeature(grad_fq, tails_after[0], short_weight[0], marks_after, doc_marks)
    grad_k = unfeature(grad_fk, tails_after[1], short_weight[1], marks_after, doc_marks)
    grad_v = unfeature(grad_fv, tails_after[2], short_weight[2], marks_after, doc_marks)
    short_term = (
        jnp.stack(
            [
                short_terms(grad_fq, q_short, short_marks, doc_marks, rim_edge),
                short_terms(grad_fk, k_short, short_marks, doc_marks, rim_edge),
                short_terms(grad_fv, v_short, short_marks, doc_marks, rim_edge),
            ]
        )
        * grad_scale
    )
    grad_short = lax.psum(short_term, "ctx")
    return (grad_q, grad_k, grad_v, grad_gain, grad_filters, grad_short)


def solution(mesh):
    return jax.shard_map(
        on_device,
        mesh=mesh,
        in_specs=(
            P("ctx", "tp"),
            P("ctx", "tp"),
            P("ctx", "tp"),
            P("ctx", "tp"),
            P("ctx"),
            P("tp"),
            P("tp", None),
            P(None, None, "tp"),
        ),
        out_specs=(
            P("ctx", "tp"),
            P("ctx", "tp"),
            P("ctx", "tp"),
            P("tp"),
            P("tp", None),
            P(None, None, "tp"),
        ),
        check_vma=False,
    )
```

profile of v0, /device:TPU:2, one launch (start us, length us, event | category | flops | bytes accessed | tf_op | source)
XLA Modules:
  0.0 352.5 jit_solution(16350759475145604191)
XLA Ops:
  8.2 3.8 %collective-permute-start.3 = (bf16[129,1024]{1,0:T(8,128)(2,1)S(1)}, bf16[129,1024]{1,0:T(8,128)(2,1)S(1)}, u32[]{:S(2)}, u32[]{:S(2)}) collective-permute-start(bf16[129,1024]{1,0:T(8,128)(2,1)S(1)} %slice.289), channel_id=1, source_target_pairs={{0,8},{8,16},{16,24},{24,32},{32,40},{40,48},{48,56},{56,64},{64,7... | collective-permute-start | bytes 792584 | tf_op jit(solution)/shard_map/ppermute | solution.py:14
  14.1 4.5 %collective-permute-start.1 = (s32[129]{0:T(256)S(1)}, s32[129]{0:T(256)S(1)}, u32[]{:S(2)}, u32[]{:S(2)}) collective-permute-start(s32[129]{0:T(256)S(1)} %slice.273), channel_id=1, source_target_pairs={{0,8},{8,16},{16,24},{24,32},{32,40},{40,48},{48,56},{56,64},{64,7... | collective-permute-start | bytes 1556 | tf_op jit(solution)/shard_map/ppermute | solution.py:14
  20.0 4.4 %collective-permute-start = (bf16[2,1024]{1,0:T(2,128)(2,1)}, bf16[2,1024]{1,0:T(2,128)(2,1)}, u32[]{:S(2)}, u32[]{:S(2)}) collective-permute-start(bf16[2,1024]{1,0:T(2,128)(2,1)} %slice.271), channel_id=1, source_target_pairs={{0,8},{8,16},{16,24},{24,32},{32,40},{40,48},{48,56},{56,64},{64,7... | collective-permute-start | bytes 12296 | tf_op jit(solution)/shard_map/ppermute | solution.py:14
  25.4 4.4 %collective-permute-start.2 = (bf16[129,1024]{1,0:T(8,128)(2,1)S(1)}, bf16[129,1024]{1,0:T(8,128)(2,1)S(1)}, u32[]{:S(2)}, u32[]{:S(2)}) collective-permute-start(bf16[129,1024]{1,0:T(8,128)(2,1)S(1)} %slice.279), channel_id=1, source_target_pairs={{0,8},{8,16},{16,24},{24,32},{32,40},{40,48},{48,56},{56,64},{64,7... | collective-permute-start | bytes 792584 | tf_op jit(solution)/shard_map/ppermute | solution.py:14
  33.2 2.6 copy.34
  38.1 16.1 %reshape.317 = bf16[64,128,255]{2,1,0:T(8,128)(2,1)} reshape(bf16[64,32640]{1,0:T(8,128)(2,1)} %slice.348) | data formatting | bytes 8355840 | tf_op jit(solution)/shard_map/reshape | solution.py:40
  55.1 2.6 copy.35
  60.0 15.9 %reshape.322 = bf16[64,128,255]{2,1,0:T(8,128)(2,1)} reshape(bf16[64,32640]{1,0:T(8,128)(2,1)} %slice.352) | data formatting | bytes 8355840 | tf_op jit(solution)/shard_map/reshape | solution.py:40
  77.7 5.0 %multiply_convert_fusion = (bf16[383,1024]{1,0:T(8,128)(2,1)S(1)}, f32[383,1024]{1,0:T(8,128)}, f32[383,1024]{1,0:T(8,128)}) fusion(f32[383]{0:T(512)S(1)} %get-tuple-element.56, f32[1024]{0:T(1024)S(1)} %bitcast.107, f32[383]{0:T(512)S(1)} %get-tuple-element.55, f32[1024]{0:T(1024)S(1)} %bitcast.109, bf16[256,1024]{1,0:T(8,128)(2,1)S(1)} %copy-done.13, ...), kind=kLoop, calls=%fused_computation.16 | loop fusion | flops 15687680 | bytes 5526520 | tf_op jit(solution)/shard_map/convert_element_type | solution.py:113
  83.3 3.6 %fusion.4 = f32[64,16,128]{2,1,0:T(8,128)S(1)} fusion(bf16[255,64,16]{0,2,1:T(8,128)(2,1)S(1)} %bitcast.78, bf16[64,128,255]{2,1,0:T(8,128)(2,1)} %reshape.317, bf16[128,255]{1,0:T(8,128)(2,1)S(1)} %get-tuple-element.70), kind=kOutput, calls=%fused_computation.8 | convolution fusion | flops 68935680 | bytes 5289728 | tf_op jit(solution)/shard_map/gij,jgc->igc/dot_general | solution.py:129
  91.2 10.7 %psum.35 = f32[256]{0:T(256)S(1)} all-reduce(f32[256]{0:T(256)} %get-tuple-element.26), channel_id=1, replica_groups=mesh['ctx'=32,'tp'=8] {'tp'}, use_global_device_ids=true, to_apply=%region_1.0 | all-reduce | flops 256 | bytes 2048 | tf_op jit(solution)/shard_map/psum | solution.py:139
  103.5 12.4 %psum.36 = f32[256]{0:T(256)S(1)} all-reduce(f32[256]{0:T(256)S(1)} %get-tuple-element.16), channel_id=1, replica_groups=mesh['ctx'=32,'tp'=8] {'tp'}, use_global_device_ids=true, to_apply=%region_3.0 | all-reduce | flops 256 | bytes 2048 | tf_op jit(solution)/shard_map/psum | solution.py:139
  122.6 5.5 %broadcast_multiply_fusion.1 = f32[64,128,255]{2,1,0:T(8,128)} fusion(f32[128,255]{1,0:T(8,128)} %get-tuple-element.59, bf16[128,64,16]{0,2,1:T(8,128)(2,1)} %bitcast.88, bf16[255,64,16]{0,2,1:T(8,128)(2,1)S(1)} %bitcast.81), kind=kOutput, calls=%fused_computation.3 | convolution fusion | flops 68935680 | bytes 9270784 | tf_op jit(solution)/shard_map/igc,jgc->gij/dot_general | solution.py:172
  128.1 9.4 %reshape.327 = f32[64,32640]{1,0:T(8,128)} reshape(f32[64,128,255]{2,1,0:T(8,128)} %broadcast_multiply_fusion.1) | data formatting | bytes 16711680 | tf_op jit(solution)/shard_map/reshape | solution.py:45
  137.5 4.0 %concatenate.58 = f32[64,32768]{1,0:T(8,128)S(1)} pad(f32[64,32640]{1,0:T(8,128)} %reshape.327, f32[]{:T(128)} %constant.19.clone.1), padding=0_0x0_128 | pad | bytes 16744452 | tf_op jit(solution)/shard_map/concatenate | solution.py:46
  147.0 5.5 %broadcast_multiply_fusion = f32[64,128,255]{2,1,0:T(8,128)} fusion(f32[128,255]{1,0:T(8,128)S(1)} %get-tuple-element.71, bf16[128,64,16]{0,2,1:T(8,128)(2,1)} %bitcast.89, bf16[255,64,16]{0,2,1:T(8,128)(2,1)S(1)} %bitcast.79), kind=kOutput, calls=%fused_computation.2 | convolution fusion | flops 68935680 | bytes 9270784 | tf_op jit(solution)/shard_map/igc,jgc->gij/dot_general | solution.py:172
  152.5 9.4 %reshape.330 = f32[64,32640]{1,0:T(8,128)} reshape(f32[64,128,255]{2,1,0:T(8,128)} %broadcast_multiply_fusion) | data formatting | bytes 16711680 | tf_op jit(solution)/shard_map/reshape | solution.py:45
  162.0 4.0 %concatenate.59 = f32[64,32768]{1,0:T(8,128)S(1)} pad(f32[64,32640]{1,0:T(8,128)} %reshape.330, f32[]{:T(128)} %constant.19.clone.1), padding=0_0x0_128 | pad | bytes 16744452 | tf_op jit(solution)/shard_map/concatenate | solution.py:46
  173.7 4.2 %fusion = f32[64,16,128]{2,1,0:T(8,128)} fusion(bf16[255,64,16]{0,2,1:T(8,128)(2,1)S(1)} %bitcast.86, bf16[64,128,255]{2,1,0:T(8,128)(2,1)} %reshape.322, bf16[128,255]{1,0:T(8,128)(2,1)S(1)} %copy-done.19), kind=kOutput, calls=%fused_computation.4 | convolution fusion | flops 68935680 | bytes 5289728 | tf_op jit(solution)/shard_map/gij,jgc->igc/dot_general | solution.py:162
  180.2 4.4 %fusion.2 = f32[64,16,128]{2,1,0:T(8,128)} fusion(bf16[255,64,16]{0,2,1:T(8,128)(2,1)} %bitcast.84, bf16[64,128,255]{2,1,0:T(8,128)(2,1)} %reshape.322, bf16[128,255]{1,0:T(8,128)(2,1)S(1)} %copy-done.18), kind=kOutput, calls=%fused_computation.6 | convolution fusion | flops 68935680 | bytes 5289728 | tf_op jit(solution)/shard_map/gij,jgc->igc/dot_general | solution.py:162
  185.9 4.1 %multiply_reduce_fusion.1 = (f32[1024]{0:T(1024)S(1)}, f32[1024]{0:T(1024)S(1)}, f32[1024]{0:T(1024)S(1)}, f32[1024]{0:T(1024)S(1)}, f32[1024]{0:T(1024)S(1)}, /...) fusion(bf16[256,1024]{1,0:T(8,128)(2,1)} %param.10, ...), kind=kLoop, calls=%fused_computation.88 | loop fusion | flops 11266048 | bytes 8165376 | tf_op jit(solution)/shard_map/reduce_sum | solution.py:74
  193.3 5.2 %collective-permute-done.6 = f32[3,2,1024]{2,1,0:T(2,128)S(1)} collective-permute-done((f32[3,2,1024]{2,1,0:T(2,128)S(1)}, f32[3,2,1024]{2,1,0:T(2,128)S(1)}, u32[]{:S(2)}, u32[]{:S(2)}) %collective-permute-start.6) | collective-permute-done | bytes 24608 | tf_op jit(solution)/shard_map/ppermute | solution.py:14
  198.7 4.0 %fusion.19 = (bf16[256,1024]{1,0:T(8,128)(2,1)}, bf16[256,1024]{1,0:T(8,128)(2,1)}) fusion(f32[256,1024]{1,0:T(8,128)} %copy-done.12, f32[2,1024]{1,0:T(2,128)S(1)} %get-tuple-element.37, f32[1024]{0:T(1024)S(1)} %bitcast.108, f32[1024]{0:T(1024)S(1)} %bitcast.110, f32[1024]{0:T(1024)S(1)} %bitcast.100, f32[256]{0:T(256)S(1)} %copy-done.45, ...), kind=kLoop, calls=%fused_computation.48 | loop fusion | flops 5242880 | bytes 3188736 | tf_op jit(solution)/shard_map/convert_element_type | solution.py:62
  203.9 137.5 %all-reduce.7.cloned.1.call-done = (f32[1024]{0:T(1024)}, f32[64,128]{1,0:T(8,128)}, f32[3,3,1024]{2,1,0:T(4,128)}) async-done(((f32[1024]{0:T(1024)}, f32[64,128]{1,0:T(8,128)}, f32[3,3,1024]{2,1,0:T(4,128)}), (f32[1024]{0:T(1024)}, f32[64,128]{1,0:T(8,128)}, f32[3,3,1024]{2,1,0:T(4,128)})) %all-reduce.7.cloned.1.call-update) | async-done | bytes 73744 | tf_op jit(solution)/shard_map/psum | solution.py:147
  (173 shorter events, 54.2 us)
Async XLA Ops:
  7.2 334.2 %all-reduce.7.cloned.1.call-start = ((), (), s32[]{:S(2)}) async-start(), calls=%async_computation | async-start | bytes 172032 | tf_op jit(solution)/shard_map/psum | solution.py:147
  8.2 69.4 %collective-permute-start.3 = (bf16[129,1024]{1,0:T(8,128)(2,1)S(1)}, bf16[129,1024]{1,0:T(8,128)(2,1)S(1)}, u32[]{:S(2)}, u32[]{:S(2)}) collective-permute-start(bf16[129,1024]{1,0:T(8,128)(2,1)S(1)} %slice.289), channel_id=1, source_target_pairs={{0,8},{8,16},{16,24},{24,32},{32,40},{40,48},{48,56},{56,64},{64,7... | collective-permute-start | bytes 792584 | tf_op jit(solution)/shard_map/ppermute | solution.py:14
  12.8 63.1 %collective-permute-start.5 = (s32[127]{0:T(128)S(1)}, s32[127]{0:T(128)S(1)}, u32[]{:S(2)}, u32[]{:S(2)}) collective-permute-start(s32[127]{0:T(128)S(1)} %slice.308), channel_id=1, source_target_pairs={{8,0},{16,8},{24,16},{32,24},{40,32},{48,40},{56,48},{64,56},{72,6... | collective-permute-start | bytes 1532 | tf_op jit(solution)/shard_map/ppermute | solution.py:14
  14.1 61.7 %collective-permute-start.1 = (s32[129]{0:T(256)S(1)}, s32[129]{0:T(256)S(1)}, u32[]{:S(2)}, u32[]{:S(2)}) collective-permute-start(s32[129]{0:T(256)S(1)} %slice.273), channel_id=1, source_target_pairs={{0,8},{8,16},{16,24},{24,32},{32,40},{40,48},{48,56},{56,64},{64,7... | collective-permute-start | bytes 1556 | tf_op jit(solution)/shard_map/ppermute | solution.py:14
  20.0 68.6 %collective-permute-start = (bf16[2,1024]{1,0:T(2,128)(2,1)}, bf16[2,1024]{1,0:T(2,128)(2,1)}, u32[]{:S(2)}, u32[]{:S(2)}) collective-permute-start(bf16[2,1024]{1,0:T(2,128)(2,1)} %slice.271), channel_id=1, source_target_pairs={{0,8},{8,16},{16,24},{24,32},{32,40},{40,48},{48,56},{56,64},{64,7... | collective-permute-start | bytes 12296 | tf_op jit(solution)/shard_map/ppermute | solution.py:14
  25.4 52.2 %collective-permute-start.2 = (bf16[129,1024]{1,0:T(8,128)(2,1)S(1)}, bf16[129,1024]{1,0:T(8,128)(2,1)S(1)}, u32[]{:S(2)}, u32[]{:S(2)}) collective-permute-start(bf16[129,1024]{1,0:T(8,128)(2,1)S(1)} %slice.279), channel_id=1, source_target_pairs={{0,8},{8,16},{16,24},{24,32},{32,40},{40,48},{48,56},{56,64},{64,7... | collective-permute-start | bytes 792584 | tf_op jit(solution)/shard_map/ppermute | solution.py:14
  31.4 46.2 %copy-start.25 = (f32[1,1,1024]{2,1,0:T(1,128)}, f32[1,1,1024]{2,1,0:T(1,128)S(1)}, u32[]{:S(2)}) copy-start(f32[1,1,1024]{2,1,0:T(1,128)S(1)} %get-tuple-element.41) | copy-start | bytes 12292
  31.4 46.2 %copy-start.27 = (f32[1,1,1024]{2,1,0:T(1,128)}, f32[1,1,1024]{2,1,0:T(1,128)S(1)}, u32[]{:S(2)}) copy-start(f32[1,1,1024]{2,1,0:T(1,128)S(1)} %get-tuple-element.42) | copy-start | bytes 12292
  31.4 46.2 %copy-start.29 = (f32[1,1,1024]{2,1,0:T(1,128)}, f32[1,1,1024]{2,1,0:T(1,128)S(1)}, u32[]{:S(2)}) copy-start(f32[1,1,1024]{2,1,0:T(1,128)S(1)} %get-tuple-element.43) | copy-start | bytes 12292
  31.4 46.2 %copy-start.31 = (f32[1,1,1024]{2,1,0:T(1,128)}, f32[1,1,1024]{2,1,0:T(1,128)S(1)}, u32[]{:S(2)}) copy-start(f32[1,1,1024]{2,1,0:T(1,128)S(1)} %get-tuple-element.44) | copy-start | bytes 12292
  31.4 46.2 %copy-start.33 = (f32[1,1,1024]{2,1,0:T(1,128)}, f32[1,1,1024]{2,1,0:T(1,128)S(1)}, u32[]{:S(2)}) copy-start(f32[1,1,1024]{2,1,0:T(1,128)S(1)} %get-tuple-element.47) | copy-start | bytes 12292
  31.4 46.2 %copy-start.35 = (f32[1,1,1024]{2,1,0:T(1,128)}, f32[1,1,1024]{2,1,0:T(1,128)S(1)}, u32[]{:S(2)}) copy-start(f32[1,1,1024]{2,1,0:T(1,128)S(1)} %get-tuple-element.48) | copy-start | bytes 12292
  38.1 16.1 %copy-start.47 = (bf16[1024]{0:T(1024)(128)(2,1)S(1)}, bf16[1024]{0:T(1024)(128)(2,1)}, u32[]{:S(2)}) copy-start(bf16[1024]{0:T(1024)(128)(2,1)} %param.13) | copy-start | bytes 6148
  60.0 16.0 %copy-start.46 = (s32[256]{0:T(256)S(1)}, s32[256]{0:T(256)}, u32[]{:S(2)}) copy-start(s32[256]{0:T(256)} %param.12) | copy-start | bytes 3076
  60.0 17.7 %copy-start.13 = (bf16[256,1024]{1,0:T(8,128)(2,1)S(1)}, bf16[256,1024]{1,0:T(8,128)(2,1)}, u32[]{:S(2)}) copy-start(bf16[256,1024]{1,0:T(8,128)(2,1)} %param.10) | copy-start | bytes 1572868
  60.0 17.7 %copy-start.14 = (bf16[256,1024]{1,0:T(8,128)(2,1)S(1)}, bf16[256,1024]{1,0:T(8,128)(2,1)}, u32[]{:S(2)}) copy-start(bf16[256,1024]{1,0:T(8,128)(2,1)} %param.9) | copy-start | bytes 1572868
  88.5 14.9 %copy-start.4 = (f32[128,1024]{1,0:T(8,128)}, f32[128,1024]{1,0:T(8,128)S(1)}, u32[]{:S(2)}) copy-start(f32[128,1024]{1,0:T(8,128)S(1)} %copy.26) | copy-start | bytes 1572868
  88.5 13.3 %copy-start.2 = (bf16[256,1024]{1,0:T(8,128)(2,1)S(1)}, bf16[256,1024]{1,0:T(8,128)(2,1)}, u32[]{:S(2)}) copy-start(bf16[256,1024]{1,0:T(8,128)(2,1)} %param.11) | copy-start | bytes 1572868
  101.8 14.0 %copy-start.39 = (f32[256]{0:T(256)}, f32[256]{0:T(256)S(1)}, u32[]{:S(2)}) copy-start(f32[256]{0:T(256)S(1)} %add_rsqrt_fusion) | copy-start | bytes 3076
  119.5 51.0 %collective-permute-start.4 = (bf16[127,1024]{1,0:T(8,128)(2,1)}, bf16[127,1024]{1,0:T(8,128)(2,1)}, u32[]{:S(2)}, u32[]{:S(2)}) collective-permute-start(bf16[127,1024]{1,0:T(8,128)(2,1)} %slice.353), channel_id=1, source_target_pairs={{8,0},{16,8},{24,16},{32,24},{40,32},{48,40},{56,48},{64,56},{72,6... | collective-permute-start | bytes 780296 | tf_op jit(solution)/shard_map/ppermute | solution.py:14
  190.0 8.6 %copy-start.26 = (f32[1,1,1024]{2,1,0:T(1,128)S(1)}, f32[1,1,1024]{2,1,0:T(1,128)}, u32[]{:S(2)}) copy-start(f32[1,1,1024]{2,1,0:T(1,128)} %copy-done.25) | copy-start | bytes 12292
  190.0 8.5 %copy-start.28 = (f32[1,1,1024]{2,1,0:T(1,128)S(1)}, f32[1,1,1024]{2,1,0:T(1,128)}, u32[]{:S(2)}) copy-start(f32[1,1,1024]{2,1,0:T(1,128)} %copy-done.27) | copy-start | bytes 12292
  190.0 8.5 %copy-start.30 = (f32[1,1,1024]{2,1,0:T(1,128)S(1)}, f32[1,1,1024]{2,1,0:T(1,128)}, u32[]{:S(2)}) copy-start(f32[1,1,1024]{2,1,0:T(1,128)} %copy-done.29) | copy-start | bytes 12292
  191.3 7.3 %collective-permute-start.6 = (f32[3,2,1024]{2,1,0:T(2,128)S(1)}, f32[3,2,1024]{2,1,0:T(2,128)S(1)}, u32[]{:S(2)}, u32[]{:S(2)}) collective-permute-start(f32[3,2,1024]{2,1,0:T(2,128)S(1)} %pad_maximum_fusion.9), channel_id=1, source_target_pairs={{8,0},{16,8},{24,16},{32,24},{40,32},{48,40},{56,48},{64,56},{72,6... | collective-permute-start | bytes 73736 | tf_op jit(solution)/shard_map/ppermute | solution.py:14
  (32 other events, 137.5 us)
Sparse Core Ops, SparseCore 0:
  193.5 147.8 all-reduce.6
where the time goes:
time: 357 us; the launch traced here: 353 us
  waiting for transfers between devices  143 us (40%)
  local copies, waits for them, and re-layouts  96.4 us (27%)
  other arithmetic  29.8 us (8%)
  matrix products  24.4 us (7%)
  blocking collectives  23.1 us (6%)
  starting transfers between devices  21 us (6%)
  between operations  15.1 us (4%)
    psum x1, waiting for transfers between devices, on_device(): grad_gain = lax.psum(gain_term, 'ctx')  137 us
    reshape x2, local copies, waits for them, and re-layouts, banded(): return repeated.reshape(groups, block_rows, span_cols)  32 us
    psum x2, blocking collectives, on_device(): lax.psum((jnp.sum(y_out * y_out, axis=1), jnp.sum(weighted * y_out, axis=...  23.1 us
    ppermute x7, starting transfers between devices, shifted(): return lax.ppermute(value, axis, pairs)  21 us
    reshape x2, local copies, waits for them, and re-layouts, diagonal_sums(): flat_terms = pair_grad.reshape(groups, block_rows * span_cols)  18.8 us
    unnamed x103, local copies, waits for them, and re-layouts  16.4 us
    dot_general x2, matrix products, on_device(): jnp.einsum('igc,jgc->gij', own_block, behind, preferred_element_type=jnp....  11 us
    dot_general x2, matrix products, on_device(): jnp.einsum('gij,jgc->igc', backward_band * agree[None], segment, preferre...  8.53 us
  transfers between devices with their start and end apart: 8, of which 2 were waited for; matrix products, arithmetic and copies ran while one was open for 33% of the time, Pallas kernels for 0%

commit v1 on v0

--- a/solution.py
+++ b/solution.py
@@ -144,7 +144,13 @@
     gain_term = (
         jnp.sum(grad_out.astype(jnp.float32) * y_out * row_scale[:, None], axis=0) * grad_scale
     )
-    grad_gain = lax.psum(gain_term, "ctx")
+    size = lax.axis_size("ctx")
+    grad_gain, stride = (gain_term, 1)
+    while stride < size:
+        grad_gain = grad_gain + lax.ppermute(
+            grad_gain, "ctx", [(i_2, i_2 ^ stride) for i_2 in range(size)]
+        )
+        stride = 2 * stride
     grad_fq = grad_y * mixed
     grad_mixed = (grad_y * feat_q).astype(jnp.bfloat16)
     following = shifted((grad_mixed[:tap_reach], doc_marks[:tap_reach]), "ctx", -1)

time: 357 us -> 369 us (1.034)
  starting transfers between devices: 21 us -> 33.9 us
    ppermute x0 -> x5, starting transfers between devices: none -> 12.9 us  [on_device(): lax.ppermute(grad_gain, 'ctx', [(i_2, i_2 ^ stride) for i_2 in range(size)])]
    unnamed x103 -> x98, local copies, waits for them, and re-layouts: 16.4 us -> 14.4 us
  transfers between devices with their start and end apart: 8 -> 13, of which waited for: 2 -> 4; matrix products, arithmetic and copies ran while one was open for 33% -> 32% of each run, Pallas kernels for 0% -> 0%
where the time goes in v1:
time: 369 us; the launch traced here: 365 us
  waiting for transfers between devices  143 us (39%)
  local copies, waits for them, and re-layouts  93.4 us (25%)
  starting transfers between devices  33.9 us (9%)
  other arithmetic  31.7 us (9%)
  matrix products  24.6 us (7%)
  blocking collectives  23.1 us (6%)
  between operations  15.1 us (4%)
    psum x1, waiting for transfers between devices, on_device(): grad_filters = lax.psum(filter_term, 'ctx')  136 us
    reshape x2, local copies, waits for them, and re-layouts, banded(): return repeated.reshape(groups, block_rows, span_cols)  32 us
    psum x2, blocking collectives, on_device(): lax.psum((jnp.sum(y_out * y_out, axis=1), jnp.sum(weighted * y_out, axis=...  23.1 us
    ppermute x7, starting transfers between devices, shifted(): return lax.ppermute(value, axis, pairs)  21 us
    reshape x2, local copies, waits for them, and re-layouts, diagonal_sums(): flat_terms = pair_grad.reshape(groups, block_rows * span_cols)  18.8 us
    unnamed x98, local copies, waits for them, and re-layouts  14.4 us
    ppermute x5, starting transfers between devices, on_device(): lax.ppermute(grad_gain, 'ctx', [(i_2, i_2 ^ stride) for i_2 in range(size)])  12.9 us
    dot_general x2, matrix products, on_device(): jnp.einsum('igc,jgc->gij', own_block, behind, preferred_element_type=jnp....  11.2 us
  transfers between devices with their start and end apart: 13, of which 4 were waited for; matrix products, arithmetic and copies ran while one was open for 32% of the time, Pallas kernels for 0%

profile of v1, /device:TPU:2, one launch (start us, length us, event | category | flops | bytes accessed | tf_op | source)
XLA Modules:
  0.0 364.5 jit_solution(7285351024216975432)
XLA Ops:
  8.2 3.8 %collective-permute-start.3 = (bf16[129,1024]{1,0:T(8,128)(2,1)S(1)}, bf16[129,1024]{1,0:T(8,128)(2,1)S(1)}, u32[]{:S(2)}, u32[]{:S(2)}) collective-permute-start(bf16[129,1024]{1,0:T(8,128)(2,1)S(1)} %slice.289), channel_id=1, source_target_pairs={{0,8},{8,16},{16,24},{24,32},{32,40},{40,48},{48,56},{56,64},{64,7... | collective-permute-start | bytes 792584 | tf_op jit(solution)/shard_map/ppermute | solution.py:14
  14.1 4.5 %collective-permute-start.1 = (s32[129]{0:T(256)S(1)}, s32[129]{0:T(256)S(1)}, u32[]{:S(2)}, u32[]{:S(2)}) collective-permute-start(s32[129]{0:T(256)S(1)} %slice.273), channel_id=1, source_target_pairs={{0,8},{8,16},{16,24},{24,32},{32,40},{40,48},{48,56},{56,64},{64,7... | collective-permute-start | bytes 1556 | tf_op jit(solution)/shard_map/ppermute | solution.py:14
  20.0 4.4 %collective-permute-start = (bf16[2,1024]{1,0:T(2,128)(2,1)}, bf16[2,1024]{1,0:T(2,128)(2,1)}, u32[]{:S(2)}, u32[]{:S(2)}) collective-permute-start(bf16[2,1024]{1,0:T(2,128)(2,1)} %slice.271), channel_id=1, source_target_pairs={{0,8},{8,16},{16,24},{24,32},{32,40},{40,48},{48,56},{56,64},{64,7... | collective-permute-start | bytes 12296 | tf_op jit(solution)/shard_map/ppermute | solution.py:14
  25.4 4.4 %collective-permute-start.2 = (bf16[129,1024]{1,0:T(8,128)(2,1)S(1)}, bf16[129,1024]{1,0:T(8,128)(2,1)S(1)}, u32[]{:S(2)}, u32[]{:S(2)}) collective-permute-start(bf16[129,1024]{1,0:T(8,128)(2,1)S(1)} %slice.279), channel_id=1, source_target_pairs={{0,8},{8,16},{16,24},{24,32},{32,40},{40,48},{48,56},{56,64},{64,7... | collective-permute-start | bytes 792584 | tf_op jit(solution)/shard_map/ppermute | solution.py:14
  38.1 16.1 %reshape.317 = bf16[64,128,255]{2,1,0:T(8,128)(2,1)} reshape(bf16[64,32640]{1,0:T(8,128)(2,1)} %slice.348) | data formatting | bytes 8355840 | tf_op jit(solution)/shard_map/reshape | solution.py:40
  60.0 15.9 %reshape.322 = bf16[64,128,255]{2,1,0:T(8,128)(2,1)} reshape(bf16[64,32640]{1,0:T(8,128)(2,1)} %slice.352) | data formatting | bytes 8355840 | tf_op jit(solution)/shard_map/reshape | solution.py:40
  77.7 4.9 %multiply_convert_fusion = (bf16[383,1024]{1,0:T(8,128)(2,1)S(1)}, f32[383,1024]{1,0:T(8,128)}, f32[383,1024]{1,0:T(8,128)}) fusion(f32[383]{0:T(512)S(1)} %get-tuple-element.55, f32[1024]{0:T(1024)S(1)} %bitcast.107, f32[383]{0:T(512)S(1)} %get-tuple-element.54, f32[1024]{0:T(1024)S(1)} %bitcast.109, bf16[256,1024]{1,0:T(8,128)(2,1)S(1)} %copy-done.12, ...), kind=kLoop, calls=%fused_computation.16 | loop fusion | flops 15687680 | bytes 5526520 | tf_op jit(solution)/shard_map/convert_element_type | solution.py:113
  83.2 3.6 fusion.4
  91.1 10.7 %psum.28 = f32[256]{0:T(256)S(1)} all-reduce(f32[256]{0:T(256)} %get-tuple-element.25), channel_id=1, replica_groups=mesh['ctx'=32,'tp'=8] {'tp'}, use_global_device_ids=true, to_apply=%region_1.0 | all-reduce | flops 256 | bytes 2048 | tf_op jit(solution)/shard_map/psum | solution.py:139
  103.4 12.4 %psum.29 = f32[256]{0:T(256)S(1)} all-reduce(f32[256]{0:T(256)S(1)} %get-tuple-element.16), channel_id=1, replica_groups=mesh['ctx'=32,'tp'=8] {'tp'}, use_global_device_ids=true, to_apply=%region_3.0 | all-reduce | flops 256 | bytes 2048 | tf_op jit(solution)/shard_map/psum | solution.py:139
  120.7 3.6 collective-permute-start.7
  125.1 5.8 %broadcast_multiply_fusion.1 = f32[64,128,255]{2,1,0:T(8,128)} fusion(f32[128,255]{1,0:T(8,128)} %get-tuple-element.58, bf16[128,64,16]{0,2,1:T(8,128)(2,1)} %bitcast.89, bf16[255,64,16]{0,2,1:T(8,128)(2,1)} %bitcast.81), kind=kOutput, calls=%fused_computation.3 | convolution fusion | flops 68935680 | bytes 9270784 | tf_op jit(solution)/shard_map/igc,jgc->gij/dot_general | solution.py:178
  135.7 5.5 %broadcast_multiply_fusion = f32[64,128,255]{2,1,0:T(8,128)} fusion(f32[128,255]{1,0:T(8,128)S(1)} %get-tuple-element.70, bf16[128,64,16]{0,2,1:T(8,128)(2,1)} %bitcast.88, bf16[255,64,16]{0,2,1:T(8,128)(2,1)S(1)} %bitcast.79), kind=kOutput, calls=%fused_computation.2 | convolution fusion | flops 68935680 | bytes 9270784 | tf_op jit(solution)/shard_map/igc,jgc->gij/dot_general | solution.py:178
  141.2 9.5 %reshape.327 = f32[64,32640]{1,0:T(8,128)} reshape(f32[64,128,255]{2,1,0:T(8,128)} %broadcast_multiply_fusion.1) | data formatting | bytes 16711680 | tf_op jit(solution)/shard_map/reshape | solution.py:45
  150.6 4.0 %concatenate.58 = f32[64,32768]{1,0:T(8,128)S(1)} pad(f32[64,32640]{1,0:T(8,128)} %reshape.327, f32[]{:T(128)} %constant.19.clone.1), padding=0_0x0_128 | pad | bytes 16744452 | tf_op jit(solution)/shard_map/concatenate | solution.py:46
  161.0 9.3 %reshape.330 = f32[64,32640]{1,0:T(8,128)} reshape(f32[64,128,255]{2,1,0:T(8,128)} %broadcast_multiply_fusion) | data formatting | bytes 16711680 | tf_op jit(solution)/shard_map/reshape | solution.py:45
  170.3 4.0 %concatenate.59 = f32[64,32768]{1,0:T(8,128)S(1)} pad(f32[64,32640]{1,0:T(8,128)} %reshape.330, f32[]{:T(128)} %constant.19.clone.1), padding=0_0x0_128 | pad | bytes 16744452 | tf_op jit(solution)/shard_map/concatenate | solution.py:46
  180.6 3.4 collective-permute-start.11
  189.6 4.2 %fusion = f32[64,16,128]{2,1,0:T(8,128)} fusion(bf16[255,64,16]{0,2,1:T(8,128)(2,1)S(1)} %bitcast.86, bf16[64,128,255]{2,1,0:T(8,128)(2,1)} %reshape.322, bf16[128,255]{1,0:T(8,128)(2,1)S(1)} %copy-done.18), kind=kOutput, calls=%fused_computation.4 | convolution fusion | flops 68935680 | bytes 5289728 | tf_op jit(solution)/shard_map/gij,jgc->igc/dot_general | solution.py:168
  196.1 4.4 %fusion.2 = f32[64,16,128]{2,1,0:T(8,128)} fusion(bf16[255,64,16]{0,2,1:T(8,128)(2,1)} %bitcast.84, bf16[64,128,255]{2,1,0:T(8,128)(2,1)} %reshape.322, bf16[128,255]{1,0:T(8,128)(2,1)S(1)} %copy-done.17), kind=kOutput, calls=%fused_computation.6 | convolution fusion | flops 68935680 | bytes 5289728 | tf_op jit(solution)/shard_map/gij,jgc->igc/dot_general | solution.py:168
  201.8 4.1 %multiply_reduce_fusion.1 = (f32[1024]{0:T(1024)S(1)}, f32[1024]{0:T(1024)S(1)}, f32[1024]{0:T(1024)S(1)}, f32[1024]{0:T(1024)S(1)}, f32[1024]{0:T(1024)S(1)}, /...) fusion(bf16[256,1024]{1,0:T(8,128)(2,1)} %param.10, ...), kind=kLoop, calls=%fused_computation.88 | loop fusion | flops 11266048 | bytes 8165376 | tf_op jit(solution)/shard_map/reduce_sum | solution.py:74
  209.3 3.7 %collective-permute-done.6 = f32[3,2,1024]{2,1,0:T(2,128)S(1)} collective-permute-done((f32[3,2,1024]{2,1,0:T(2,128)S(1)}, f32[3,2,1024]{2,1,0:T(2,128)S(1)}, u32[]{:S(2)}, u32[]{:S(2)}) %collective-permute-start.6) | collective-permute-done | bytes 24608 | tf_op jit(solution)/shard_map/ppermute | solution.py:14
  213.1 3.9 %fusion.19 = (bf16[256,1024]{1,0:T(8,128)(2,1)}, bf16[256,1024]{1,0:T(8,128)(2,1)}) fusion(f32[256,1024]{1,0:T(8,128)} %copy-done.11, f32[2,1024]{1,0:T(2,128)S(1)} %get-tuple-element.36, f32[1024]{0:T(1024)S(1)} %bitcast.108, f32[1024]{0:T(1024)S(1)} %bitcast.110, f32[1024]{0:T(1024)S(1)} %bitcast.100, f32[256]{0:T(256)S(1)} %copy-done.43, ...), kind=kLoop, calls=%fused_computation.48 | loop fusion | flops 5242880 | bytes 3188736 | tf_op jit(solution)/shard_map/convert_element_type | solution.py:62
  218.3 136.4 %all-reduce.7.cloned.1.call-done = (f32[64,128]{1,0:T(8,128)}, f32[3,3,1024]{2,1,0:T(4,128)}) async-done(((f32[64,128]{1,0:T(8,128)}, f32[3,3,1024]{2,1,0:T(4,128)}), (f32[64,128]{1,0:T(8,128)}, f32[3,3,1024]{2,1,0:T(4,128)})) %all-reduce.7.cloned.1.call-update) | async-done | bytes 69648 | tf_op jit(solution)/shard_map/psum | solution.py:183
  (183 shorter events, 67.0 us)
Async XLA Ops:
  7.2 347.5 %all-reduce.7.cloned.1.call-start = ((), (), s32[]{:S(2)}) async-start(), calls=%async_computation | async-start | bytes 163840 | tf_op jit(solution)/shard_map/psum | solution.py:183
  8.2 69.4 %collective-permute-start.3 = (bf16[129,1024]{1,0:T(8,128)(2,1)S(1)}, bf16[129,1024]{1,0:T(8,128)(2,1)S(1)}, u32[]{:S(2)}, u32[]{:S(2)}) collective-permute-start(bf16[129,1024]{1,0:T(8,128)(2,1)S(1)} %slice.289), channel_id=1, source_target_pairs={{0,8},{8,16},{16,24},{24,32},{32,40},{40,48},{48,56},{56,64},{64,7... | collective-permute-start | bytes 792584 | tf_op jit(solution)/shard_map/ppermute | solution.py:14
  12.8 63.1 %collective-permute-start.5 = (s32[127]{0:T(128)S(1)}, s32[127]{0:T(128)S(1)}, u32[]{:S(2)}, u32[]{:S(2)}) collective-permute-start(s32[127]{0:T(128)S(1)} %slice.308), channel_id=1, source_target_pairs={{8,0},{16,8},{24,16},{32,24},{40,32},{48,40},{56,48},{64,56},{72,6... | collective-permute-start | bytes 1532 | tf_op jit(solution)/shard_map/ppermute | solution.py:14
  14.1 61.8 %collective-permute-start.1 = (s32[129]{0:T(256)S(1)}, s32[129]{0:T(256)S(1)}, u32[]{:S(2)}, u32[]{:S(2)}) collective-permute-start(s32[129]{0:T(256)S(1)} %slice.273), channel_id=1, source_target_pairs={{0,8},{8,16},{16,24},{24,32},{32,40},{40,48},{48,56},{56,64},{64,7... | collective-permute-start | bytes 1556 | tf_op jit(solution)/shard_map/ppermute | solution.py:14
  20.0 68.5 %collective-permute-start = (bf16[2,1024]{1,0:T(2,128)(2,1)}, bf16[2,1024]{1,0:T(2,128)(2,1)}, u32[]{:S(2)}, u32[]{:S(2)}) collective-permute-start(bf16[2,1024]{1,0:T(2,128)(2,1)} %slice.271), channel_id=1, source_target_pairs={{0,8},{8,16},{16,24},{24,32},{32,40},{40,48},{48,56},{56,64},{64,7... | collective-permute-start | bytes 12296 | tf_op jit(solution)/shard_map/ppermute | solution.py:14
  25.4 52.2 %collective-permute-start.2 = (bf16[129,1024]{1,0:T(8,128)(2,1)S(1)}, bf16[129,1024]{1,0:T(8,128)(2,1)S(1)}, u32[]{:S(2)}, u32[]{:S(2)}) collective-permute-start(bf16[129,1024]{1,0:T(8,128)(2,1)S(1)} %slice.279), channel_id=1, source_target_pairs={{0,8},{8,16},{16,24},{24,32},{32,40},{40,48},{48,56},{56,64},{64,7... | collective-permute-start | bytes 792584 | tf_op jit(solution)/shard_map/ppermute | solution.py:14
  31.4 46.2 %copy-start.23 = (f32[1,1,1024]{2,1,0:T(1,128)}, f32[1,1,1024]{2,1,0:T(1,128)S(1)}, u32[]{:S(2)}) copy-start(f32[1,1,1024]{2,1,0:T(1,128)S(1)} %get-tuple-element.40) | copy-start | bytes 12292
  31.4 46.3 %copy-start.25 = (f32[1,1,1024]{2,1,0:T(1,128)}, f32[1,1,1024]{2,1,0:T(1,128)S(1)}, u32[]{:S(2)}) copy-start(f32[1,1,1024]{2,1,0:T(1,128)S(1)} %get-tuple-element.41) | copy-start | bytes 12292
  31.4 46.3 %copy-start.27 = (f32[1,1,1024]{2,1,0:T(1,128)}, f32[1,1,1024]{2,1,0:T(1,128)S(1)}, u32[]{:S(2)}) copy-start(f32[1,1,1024]{2,1,0:T(1,128)S(1)} %get-tuple-element.42) | copy-start | bytes 12292
  31.4 46.3 %copy-start.29 = (f32[1,1,1024]{2,1,0:T(1,128)}, f32[1,1,1024]{2,1,0:T(1,128)S(1)}, u32[]{:S(2)}) copy-start(f32[1,1,1024]{2,1,0:T(1,128)S(1)} %get-tuple-element.43) | copy-start | bytes 12292
  31.4 46.3 %copy-start.31 = (f32[1,1,1024]{2,1,0:T(1,128)}, f32[1,1,1024]{2,1,0:T(1,128)S(1)}, u32[]{:S(2)}) copy-start(f32[1,1,1024]{2,1,0:T(1,128)S(1)} %get-tuple-element.46) | copy-start | bytes 12292
  31.4 46.3 %copy-start.33 = (f32[1,1,1024]{2,1,0:T(1,128)}, f32[1,1,1024]{2,1,0:T(1,128)S(1)}, u32[]{:S(2)}) copy-start(f32[1,1,1024]{2,1,0:T(1,128)S(1)} %get-tuple-element.47) | copy-start | bytes 12292
  38.1 16.1 %copy-start.45 = (bf16[1024]{0:T(1024)(128)(2,1)S(1)}, bf16[1024]{0:T(1024)(128)(2,1)}, u32[]{:S(2)}) copy-start(bf16[1024]{0:T(1024)(128)(2,1)} %param.13) | copy-start | bytes 6148
  60.0 16.0 %copy-start.44 = (s32[256]{0:T(256)S(1)}, s32[256]{0:T(256)}, u32[]{:S(2)}) copy-start(s32[256]{0:T(256)} %param.12) | copy-start | bytes 3076
  60.0 17.7 %copy-start.12 = (bf16[256,1024]{1,0:T(8,128)(2,1)S(1)}, bf16[256,1024]{1,0:T(8,128)(2,1)}, u32[]{:S(2)}) copy-start(bf16[256,1024]{1,0:T(8,128)(2,1)} %param.10) | copy-start | bytes 1572868
  60.0 17.7 %copy-start.13 = (bf16[256,1024]{1,0:T(8,128)(2,1)S(1)}, bf16[256,1024]{1,0:T(8,128)(2,1)}, u32[]{:S(2)}) copy-start(bf16[256,1024]{1,0:T(8,128)(2,1)} %param.9) | copy-start | bytes 1572868
  88.5 14.9 %copy-start.4 = (f32[128,1024]{1,0:T(8,128)}, f32[128,1024]{1,0:T(8,128)S(1)}, u32[]{:S(2)}) copy-start(f32[128,1024]{1,0:T(8,128)S(1)} %copy.26) | copy-start | bytes 1572868
  118.8 67.7 %collective-permute-start.4 = (bf16[127,1024]{1,0:T(8,128)(2,1)}, bf16[127,1024]{1,0:T(8,128)(2,1)}, u32[]{:S(2)}, u32[]{:S(2)}) collective-permute-start(bf16[127,1024]{1,0:T(8,128)(2,1)} %slice.353), channel_id=1, source_target_pairs={{8,0},{16,8},{24,16},{32,24},{40,32},{48,40},{56,48},{64,56},{72,6... | collective-permute-start | bytes 780296 | tf_op jit(solution)/shard_map/ppermute | solution.py:14
  120.7 12.0 %collective-permute-start.7 = (f32[1024]{0:T(1024)}, f32[1024]{0:T(1024)}, u32[]{:S(2)}, u32[]{:S(2)}) collective-permute-start(f32[1024]{0:T(1024)} %broadcast_multiply_fusion.3), channel_id=1, source_target_pairs={{0,8},{8,0},{16,24},{24,16},{32,40},{40,32},{48,56},{56,48},{64,72... | collective-permute-start | bytes 12296 | tf_op jit(solution)/shard_map/ppermute | solution.py:150
  134.0 23.2 %collective-permute-start.8 = (f32[1024]{0:T(1024)}, f32[1024]{0:T(1024)}, u32[]{:S(2)}, u32[]{:S(2)}) collective-permute-start(f32[1024]{0:T(1024)} %fusion.68), channel_id=1, source_target_pairs={{0,16},{8,24},{16,0},{24,8},{32,48},{40,56},{48,32},{56,40},{64,80... | collective-permute-start | bytes 12296 | tf_op jit(solution)/shard_map/ppermute | solution.py:150
  157.9 19.0 %collective-permute-start.9 = (f32[1024]{0:T(1024)S(1)}, f32[1024]{0:T(1024)S(1)}, u32[]{:S(2)}, u32[]{:S(2)}) collective-permute-start(f32[1024]{0:T(1024)S(1)} %add.99), channel_id=1, source_target_pairs={{0,32},{8,40},{16,48},{24,56},{32,0},{40,8},{48,16},{56,24},{64,96... | collective-permute-start | bytes 12296 | tf_op jit(solution)/shard_map/ppermute | solution.py:150
  176.9 3.7 %collective-permute-start.10 = (f32[1024]{0:T(1024)S(1)}, f32[1024]{0:T(1024)S(1)}, u32[]{:S(2)}, u32[]{:S(2)}) collective-permute-start(f32[1024]{0:T(1024)S(1)} %add.100), channel_id=1, source_target_pairs={{0,64},{8,72},{16,80},{24,88},{32,96},{40,104},{48,112},{56,120},{... | collective-permute-start | bytes 12296 | tf_op jit(solution)/shard_map/ppermute | solution.py:150
  180.6 5.3 %collective-permute-start.11 = (f32[1024]{0:T(1024)S(1)}, f32[1024]{0:T(1024)S(1)}, u32[]{:S(2)}, u32[]{:S(2)}) collective-permute-start(f32[1024]{0:T(1024)S(1)} %add.101), channel_id=1, source_target_pairs={{0,128},{8,136},{16,144},{24,152},{32,160},{40,168},{48,176},{56,1... | collective-permute-start | bytes 12296 | tf_op jit(solution)/shard_map/ppermute | solution.py:150
  207.2 5.7 %collective-permute-start.6 = (f32[3,2,1024]{2,1,0:T(2,128)S(1)}, f32[3,2,1024]{2,1,0:T(2,128)S(1)}, u32[]{:S(2)}, u32[]{:S(2)}) collective-permute-start(f32[3,2,1024]{2,1,0:T(2,128)S(1)} %pad_maximum_fusion.9), channel_id=1, source_target_pairs={{8,0},{16,8},{24,16},{32,24},{40,32},{48,40},{56,48},{64,56},{72,6... | collective-permute-start | bytes 73736 | tf_op jit(solution)/shard_map/ppermute | solution.py:14
  (35 other events, 184.7 us)
Sparse Core Ops, SparseCore 0:
  209.4 145.2 all-reduce.6
